TPU v7x, 512 devices: a whole 4x4x16 slice. The times are simulated.
512 devices in a mesh: rows: 64 (over y, z), cols: 8 (over x, core).
Axes of the slice: x: 4, y: 4, z: 16, core: 2. Of those that a mesh axis runs over, the one named last changes fastest.
Arguments:
- node_features: bfloat16 [65536, 512], P('rows', 'cols'), may hold values from -6 to 6
- weight: bfloat16 [512, 512], replicated, may hold values from -0.25 to 0.25
- tile_values: bfloat16 [4096, 128, 128], P('rows'), may hold values from -0.1875 to 0.1875
- tile_row: int32 [4096], P('rows'), may hold values from 0 to 7
- source_owner: int32 [4096, 1], P('rows'), may hold values from 0 to 63; in each aligned block of 64 rows (0 to 63, 64 to 127, ...) at most 2 rows name the same one
- source_block: int32 [4096], P('rows'), may hold values from 0 to 7
- labels: int32 [65536], P('rows'), may hold values from 0 to 511
Outputs:
- activations: bfloat16 [65536, 512], P('rows', 'cols')
- weight_grad: float32 [512, 512], P(None, 'cols')
- feature_grad: bfloat16 [65536, 512], P('rows', 'cols')
Inputs may be any that keep to these rules, and one draw needn't show every extreme that they name: `source_owner`: of the 64 tiles of one index of rows, at most 2 name the same owner.
All inputs are finite; a program needn't handle non-finite values.
Results may differ from a plain program's by a relative error of at most 0.0095.
Values may be sent and summed in bfloat16 or wider, within the bound.
A program may use at most 64 MiB of HBM per device.

v0:
```python
import math
import jax
import jax.numpy as jnp
from jax import lax
from jax.sharding import PartitionSpec as P


def slot_ranks(owners):
    positions = jnp.arange(owners.shape[0], dtype=jnp.int32)
    earlier = (owners[:, None] == owners[None, :]) & (positions[None, :] < positions[:, None])
    return jnp.sum(earlier.astype(jnp.int32), axis=1)


def per_device(node_features, weight, tile_values, tile_row, source_owner, source_block, labels):
    local_rows, col_width = node_features.shape
    block_size = tile_values.shape[1]
    local_blocks = local_rows // block_size
    row_devices = lax.axis_size("rows")
    capacity = 2 * tile_values.shape[0] // row_devices
    owners = source_owner[:, 0]
    slot_rank = slot_ranks(owners)
    column_block = owners * local_blocks + source_block
    local_ids = jnp.arange(local_blocks, dtype=jnp.int32)
    row_onehot = (tile_row[:, None] == local_ids[None, :]).astype(jnp.float32)
    gathered = lax.all_gather(node_features, "rows", axis=0, tiled=True)
    all_blocks = gathered.reshape(row_devices * local_blocks, block_size, col_width)
    source_rows = all_blocks[column_block]
    products = jnp.einsum(
        "tij,tjf->tif", tile_values, source_rows, preferred_element_type=jnp.float32
    )
    summed = jnp.einsum("tb,tif->bif", row_onehot, products, precision=lax.Precision.HIGHEST)
    aggregated = summed.reshape(local_rows, col_width).astype(jnp.bfloat16)
    aggregated_all = lax.all_gather(aggregated, "cols", axis=1, tiled=True)
    col_index = lax.axis_index("cols")
    w_columns = lax.dynamic_slice_in_dim(weight, col_index * col_width, col_width, 1)
    w_rows = lax.dynamic_slice_in_dim(weight, col_index * col_width, col_width, 0)
    hidden = jnp.dot(aggregated_all, w_columns, preferred_element_type=jnp.float32)
    sigmoid = jax.nn.sigmoid(hidden)
    activated = hidden * sigmoid
    slopes = sigmoid * (1.0 + hidden * (1.0 - sigmoid))
    feature_ids = col_index * col_width + jnp.arange(col_width, dtype=jnp.int32)
    target = (labels[:, None] == feature_ids[None, :]).astype(jnp.float32)
    out_grad = ((activated - target) * slopes).astype(jnp.bfloat16)
    grad_all = lax.all_gather(out_grad, "cols", axis=1, tiled=True)
    weight_terms = jnp.einsum(
        "nk,nc->kc", aggregated_all, out_grad, preferred_element_type=jnp.float32
    )
    node_total = local_rows * row_devices
    weight_grad = lax.psum(weight_terms, "rows") / math.sqrt(node_total)
    agg_grad = jnp.einsum("nc,kc->nk", grad_all, w_rows, preferred_element_type=jnp.float32).astype(
        jnp.bfloat16
    )
    grad_rows = agg_grad.reshape(local_blocks, block_size, col_width)[tile_row]
    sent_terms = jnp.einsum(
        "tji,tjf->tif", tile_values, grad_rows, preferred_element_type=jnp.float32
    )
    send_terms = (
        jnp.zeros((row_devices, capacity, block_size, col_width), jnp.float32)
        .at[owners, slot_rank]
        .set(sent_terms)
    )
    send_index = (
        jnp.zeros((row_devices, capacity), jnp.int32).at[owners, slot_rank].set(source_block)
    )
    received, recv_index = (
        lax.all_to_all(
            send_terms.astype(jnp.bfloat16), "rows", split_axis=0, concat_axis=0, tiled=True
        ).astype(send_terms.dtype),
        lax.all_to_all(send_index, "rows", split_axis=0, concat_axis=0, tiled=True),
    )
    placing = (recv_index[:, :, None] == local_ids[None, None, :]).astype(jnp.float32)
    filled = (jnp.abs(received).sum(axis=(2, 3)) >= 0.0).astype(jnp.float32)
    feature_grad = jnp.einsum(
        "scb,scif->bif", placing * filled[:, :, None], received, precision=lax.Precision.HIGHEST
    ).reshape(local_rows, col_width)
    return (activated.astype(jnp.bfloat16), weight_grad, feature_grad.astype(jnp.bfloat16))


def solution(mesh):
    return jax.shard_map(
        per_device,
        mesh=mesh,
        in_specs=(
            P("rows", "cols"),
            P(),
            P("rows", None, None),
            P("rows"),
            P("rows", None),
            P("rows"),
            P("rows"),
        ),
        out_specs=(P("rows", "cols"), P(None, "cols"), P("rows", "cols")),
        check_vma=False,
    )
```

profile of v0, /device:TPU:2, one launch (start us, length us, event | category | flops | bytes accessed | tf_op | source)
XLA Modules:
  0.0 590.2 jit_solution(7779311799218977783)
XLA Ops:
  7.2 0.0 copy-start
  7.2 0.0 all-gather.4.cloned.1.call-start
  7.2 0.7 all-gather.4.cloned.1.call-update
  7.9 0.0 all-gather.6.cloned.1.call-start
  8.0 0.7 compare_select_fusion.3
  8.6 164.2 %all-gather.4.cloned.1.call-done = bf16[65536,64]{0,1:T(8,128)(2,1)} async-done(((bf16[1024,64]{0,1:T(8,128)(2,1)}), bf16[65536,64]{0,1:T(8,128)(2,1)}) %all-gather.4.cloned.1.call-update) | async-done | bytes 8388624 | tf_op jit(solution)/shard_map/all_gather | solution.py:25
  172.9 9.0 %copy_bitcast_fusion = bf16[512,128,64]{1,2,0:T(8,128)(2,1)} fusion(bf16[65536,64]{0,1:T(8,128)(2,1)} %all-gather.4.cloned.1.call-done), kind=kLoop, calls=%fused_computation.4 | loop fusion | bytes 16777216 | tf_op jit(solution)/shard_map/reshape | solution.py:26
  181.9 4.1 gather_fusion
  186.0 0.0 copy-start.4
  186.0 1.5 convolution_bitcast_fusion.1
  187.6 0.0 copy-start.5
  187.6 2.0 fusion.10
  189.6 0.0 copy-start.6
  189.6 0.0 copy-start.3
  189.6 0.7 copy.68
  190.3 0.0 all-gather.6.cloned.1.call-update
  190.3 0.0 all-gather.8.cloned.1.call-start
  190.4 24.7 %all-gather.6.cloned.1.call-done = bf16[1024,512]{0,1:T(8,128)(2,1)} async-done(((bf16[1024,64]{0,1:T(8,128)(2,1)}), bf16[1024,512]{0,1:T(8,128)(2,1)}) %all-gather.6.cloned.1.call-update) | async-done | bytes 1048592 | tf_op jit(solution)/shard_map/all_gather | solution.py:33
  215.0 0.0 copy-done.5
  215.0 2.4 multiply_convert_fusion
  217.4 0.0 all-gather.8.cloned.1.call-update
  217.5 0.2 convert_reduce_fusion
  217.7 3.5 scatter_fusion
  221.2 0.7 copy.42
  221.9 15.2 %all-to-all-start = ((s32[64,1,2]{2,1,0:T(1,128)}), s32[64,1,2]{2,1,0:T(1,128)S(1)}, u32[]{:S(2)}, u32[]{:S(2)}) async-start(s32[64,1,2]{2,1,0:T(1,128)} %copy.42), calls=%async_computation | async-start | bytes 65536 | tf_op jit(solution)/shard_map/all_to_all | solution.py:69
  237.1 11.6 %all-gather.8.cloned.1.call-done = bf16[1024,512]{0,1:T(8,128)(2,1)} async-done(((bf16[1024,64]{0,1:T(8,128)(2,1)}), bf16[1024,512]{0,1:T(8,128)(2,1)}) %all-gather.8.cloned.1.call-update) | async-done | bytes 1048592 | tf_op jit(solution)/shard_map/all_gather | solution.py:44
  248.7 1.6 fusion.13
  250.3 0.8 gather_fusion.1
  251.1 2.0 convolution_bitcast_fusion
  253.1 2.5 broadcast_in_dim.10
  255.6 10.6 %scatter_fusion.1 = f32[64,2,128,64]{2,3,1,0:T(8,128)} fusion(f32[64,2,128,64]{2,3,1,0:T(8,128)} %broadcast_in_dim.10, s32[64]{0:T(128)S(1)} %fusion.31, f32[64,128,64]{1,2,0:T(8,128)} %convolution_bitcast_fusion), kind=kCustom, calls=%fused_computation.3 | custom fusion | bytes 6291968 | tf_op jit(solution)/shard_map/scatter | solution.py:60
  266.2 2.7 convert_element_type.49
  268.9 3.5 copy.45
  272.4 0.0 all-to-all-done
  272.4 15.9 %all-to-all-start.1 = ((bf16[64,2,128,64]{2,1,3,0:T(2,128)(2,1)}), bf16[64,2,128,64]{2,1,3,0:T(2,128)(2,1)}, u32[]{:S(2)}, u32[]{:S(2)}) async-start(bf16[64,2,128,64]{2,1,3,0:T(2,128)(2,1)} %copy.45), calls=%async_computation.1 | async-start | bytes 4194304 | tf_op jit(solution)/shard_map/all_to_all | solution.py:66
  288.4 0.0 all-reduce.2.cloned.1.call-start
  288.4 0.0 copy-done.1
  288.4 0.0 copy-done.2
  288.4 1.1 fusion.33
  289.5 0.0 all-reduce.2.cloned.1.call-update
  289.6 0.1 copy.43
  289.6 283.3 %all-reduce.2.cloned.1.call-done = f32[512,64]{0,1:T(8,128)} async-done(((f32[512,64]{0,1:T(8,128)}), f32[512,64]{0,1:T(8,128)}) %all-reduce.2.cloned.1.call-update) | async-done | bytes 131088 | tf_op jit(solution)/shard_map/psum | solution.py:49
  573.0 1.6 broadcast_multiply_fusion
  574.5 0.0 all-to-all-done.1
  574.5 3.8 abs_reduce_fusion
  578.4 0.1 copy.46
  578.5 4.5 fusion.7
  583.0 0.7 copy.67
  (14 shorter events, 0.1 us)
Async XLA Ops:
  7.2 178.9 %copy-start = (bf16[64,128,128]{2,1,0:T(8,128)(2,1)S(1)}, bf16[64,128,128]{2,1,0:T(8,128)(2,1)}, u32[]{:S(2)}) copy-start(bf16[64,128,128]{2,1,0:T(8,128)(2,1)} %param.9) | copy-start | bytes 6291460
  7.2 165.7 %all-gather.4.cloned.1.call-start = ((), (), s32[]{:S(2)}) async-start(), calls=%async_computation.2 | async-start | bytes 8519680 | tf_op jit(solution)/shard_map/all_gather | solution.py:25
  7.9 207.1 %all-gather.6.cloned.1.call-start = ((), (), s32[]{:S(2)}) async-start(), calls=%async_computation.3 | async-start | bytes 1179648 | tf_op jit(solution)/shard_map/all_gather | solution.py:33
  186.0 1.5 copy-start.4
  187.6 27.4 %copy-start.5 = (s32[1024]{0:T(1024)S(1)}, s32[1024]{0:T(1024)}, u32[]{:S(2)}) copy-start(s32[1024]{0:T(1024)} %param.13) | copy-start | bytes 12292
  189.6 27.9 %copy-start.6 = (s32[64,1]{0,1:T(1,128)S(1)}, s32[64,1]{0,1:T(1,128)}, u32[]{:S(2)}) copy-start(s32[64,1]{0,1:T(1,128)} %param.11) | copy-start | bytes 772
  189.6 28.1 %copy-start.3 = (s32[64]{0:T(128)S(1)}, s32[64]{0:T(128)}, u32[]{:S(2)}) copy-start(s32[64]{0:T(128)} %param.12) | copy-start | bytes 772
  190.3 58.4 %all-gather.8.cloned.1.call-start = ((), (), s32[]{:S(2)}) async-start(), calls=%async_computation.5 | async-start | bytes 1179648 | tf_op jit(solution)/shard_map/all_gather | solution.py:44
  221.9 50.5 %all-to-all-start = ((s32[64,1,2]{2,1,0:T(1,128)}), s32[64,1,2]{2,1,0:T(1,128)S(1)}, u32[]{:S(2)}, u32[]{:S(2)}) async-start(s32[64,1,2]{2,1,0:T(1,128)} %copy.42), calls=%async_computation | async-start | bytes 65536 | tf_op jit(solution)/shard_map/all_to_all | solution.py:69
  272.4 16.0 %copy-start.1 = (bf16[1024,512]{0,1:T(8,128)(2,1)S(1)}, bf16[1024,512]{0,1:T(8,128)(2,1)}, u32[]{:S(2)}) copy-start(bf16[1024,512]{0,1:T(8,128)(2,1)} %all-gather.6.cloned.1.call-done) | copy-start | bytes 3145732
  272.4 16.0 %copy-start.2 = (bf16[1024,64]{0,1:T(8,128)(2,1)S(1)}, bf16[1024,64]{0,1:T(8,128)(2,1)}, u32[]{:S(2)}) copy-start(bf16[1024,64]{0,1:T(8,128)(2,1)} %get-tuple-element.3) | copy-start | bytes 393220
  272.4 302.1 %all-to-all-start.1 = ((bf16[64,2,128,64]{2,1,3,0:T(2,128)(2,1)}), bf16[64,2,128,64]{2,1,3,0:T(2,128)(2,1)}, u32[]{:S(2)}, u32[]{:S(2)}) async-start(bf16[64,2,128,64]{2,1,3,0:T(2,128)(2,1)} %copy.45), calls=%async_computation.1 | async-start | bytes 4194304 | tf_op jit(solution)/shard_map/all_to_all | solution.py:66
  288.4 284.6 %all-reduce.2.cloned.1.call-start = ((), (), s32[]{:S(2)}) async-start(), calls=%async_computation.4 | async-start | bytes 262144 | tf_op jit(solution)/shard_map/psum | solution.py:49
Sparse Core Ops, SparseCore 0:
  11.0 161.8 all-gather.3
  190.4 24.5 all-gather.5
  217.7 30.9 all-gather.7
  292.9 280.0 all-reduce.1
where the time goes:
time: 591 us; the launch traced here: 590 us
  waiting for transfers between devices  485 us (82%)
  local copies, waits for them, and re-layouts  36.3 us (6%)
  starting transfers between devices  31.3 us (5%)
  matrix products  15.1 us (3%)
  between operations  14 us (2%)
  other arithmetic  9.01 us (2%)
    psum x1, waiting for transfers between devices, per_device(): weight_grad = lax.psum(weight_terms, 'rows') / math.sqrt(node_total)  283 us
    all_gather x1, waiting for transfers between devices, per_device(): gathered = lax.all_gather(node_features, 'rows', axis=0, tiled=True)  164 us
    all_gather x1, waiting for transfers between devices, per_device(): aggregated_all = lax.all_gather(aggregated, 'cols', axis=1, tiled=True)  24.7 us
    all_to_all x1, starting transfers between devices, per_device(): lax.all_to_all(send_terms.astype(jnp.bfloat16), 'rows', split_axis=0, con...  15.9 us
    all_to_all x1, starting transfers between devices, per_device(): lax.all_to_all(send_index, 'rows', split_axis=0, concat_axis=0, tiled=True)  15.2 us
  transfers between devices with their start and end apart: 6, of which 4 were waited for; matrix products, arithmetic and copies ran while one was open for 5% of the time, Pallas kernels for 0%

commit v1 on v0

--- a/solution.py
+++ b/solution.py
@@ -22,7 +22,13 @@
     column_block = owners * local_blocks + source_block
     local_ids = jnp.arange(local_blocks, dtype=jnp.int32)
     row_onehot = (tile_row[:, None] == local_ids[None, :]).astype(jnp.float32)
-    gathered = lax.all_gather(node_features, "rows", axis=0, tiled=True)
+    entries = []
+    for _ in range(lax.axis_size("rows")):
+        entries.append(node_features)
+    gathered = jnp.concatenate(
+        lax.all_to_all(jnp.stack(entries, axis=0), axis_name="rows", split_axis=0, concat_axis=0),
+        axis=0,
+    )
     all_blocks = gathered.reshape(row_devices * local_blocks, block_size, col_width)
     source_rows = all_blocks[column_block]
     products = jnp.einsum(

time: 591 us -> 844 us (1.43)
  waiting for transfers between devices: 485 us -> 686 us
  local copies, waits for them, and re-layouts: 36.3 us -> 69.5 us
  starting transfers between devices: 31.3 us -> 50.4 us
    all_to_all x0 -> x1, waiting for transfers between devices: none -> 368 us  [per_device(): lax.all_to_all(jnp.stack(entries, axis=0), axis_name='rows', split_axis=0...]
    all_gather x1 -> x0, waiting for transfers between devices: 164 us -> none  [per_device(): gathered = lax.all_gather(node_features, 'rows', axis=0, tiled=True)]
    another operation x0 -> x3, local copies, waits for them, and re-layouts: none -> 30.8 us  [the longest x2 25.4 us: per_device(): gathered.reshape(row_devices * local_blocks, block_size, col_width)]
    all_to_all x0 -> x1, starting transfers between devices: none -> 19.1 us  [per_device(): lax.all_to_all(jnp.stack(entries, axis=0), axis_name='rows', split_axis=0...]
    all_to_all x0 -> x1, local copies, waits for them, and re-layouts: none -> 11.3 us  [per_device(): lax.all_to_all(jnp.stack(entries, axis=0), axis_name='rows', split_axis=0...]
    reshape x1 -> x0, local copies, waits for them, and re-layouts: 9.04 us -> none  [per_device(): gathered.reshape(row_devices * local_blocks, block_size, col_width)]
  transfers between devices with their start and end apart: 6 -> 6, of which waited for: 4 -> 4; matrix products, arithmetic and copies ran while one was open for 5% -> 4% of each run, Pallas kernels for 0% -> 0%
where the time goes in v1:
time: 844 us; the launch traced here: 843 us
  waiting for transfers between devices  686 us (81%)
  local copies, waits for them, and re-layouts  69.5 us (8%)
  starting transfers between devices  50.4 us (6%)
  matrix products  15.1 us (2%)
  between operations  13.9 us (2%)
    all_to_all x1, waiting for transfers between devices, per_device(): lax.all_to_all(jnp.stack(entries, axis=0), axis_name='rows', split_axis=0...  368 us
    psum x1, waiting for transfers between devices, per_device(): weight_grad = lax.psum(weight_terms, 'rows') / math.sqrt(node_total)  284 us
    another operation x2, local copies, waits for them, and re-layouts, per_device(): gathered.reshape(row_devices * local_blocks, block_size, col_width)  25.4 us
    all_gather x1, waiting for transfers between devices, per_device(): aggregated_all = lax.all_gather(aggregated, 'cols', axis=1, tiled=True)  23 us
    all_to_all x1, starting transfers between devices, per_device(): lax.all_to_all(jnp.stack(entries, axis=0), axis_name='rows', split_axis=0...  19.1 us
  transfers between devices with their start and end apart: 6, of which 4 were waited for; matrix products, arithmetic and copies ran while one was open for 4% of the time, Pallas kernels for 0%

profile of v1, /device:TPU:2, one launch (start us, length us, event | category | flops | bytes accessed | tf_op | source)
XLA Modules:
  0.0 843.3 jit_solution(3870111000933753153)
XLA Ops:
  7.2 0.0 copy-start
  7.2 5.4 stack.2
  12.5 19.1 %all-to-all-start = ((bf16[64,1024,64]{1,2,0:T(8,128)(2,1)}), bf16[64,1024,64]{1,2,0:T(8,128)(2,1)}, u32[]{:S(2)}, u32[]{:S(2)}) async-start(bf16[64,1024,64]{1,2,0:T(8,128)(2,1)} %stack.2), calls=%async_computation | async-start | bytes 16777216 | tf_op jit(solution)/shard_map/all_to_all | solution.py:29
  31.7 0.0 all-gather.3.cloned.1.call-start
  31.7 0.0 copy-done.3
  31.7 0.0 copy-done.6
  31.8 367.6 %all-to-all-done = bf16[64,1024,64]{1,2,0:T(8,128)(2,1)} async-done(((bf16[64,1024,64]{1,2,0:T(8,128)(2,1)}), bf16[64,1024,64]{1,2,0:T(8,128)(2,1)}, u32[]{:S(2)}, u32[]{:S(2)}) %all-to-all-start) | async-done | bytes 8388640 | tf_op jit(solution)/shard_map/all_to_all | solution.py:29
  399.4 11.3 %copy.47 = bf16[64,1024,64]{1,0,2:T(8,128)(2,1)} copy(bf16[64,1024,64]{1,2,0:T(8,128)(2,1)} %all-to-all-done) | data formatting | bytes 16777216 | tf_op jit(solution)/shard_map/all_to_all | solution.py:29
  410.7 13.4 %reshape_reshape.3 = bf16[512,128,64]{1,0,2:T(8,128)(2,1)} reshape(bf16[64,1024,64]{1,0,2:T(8,128)(2,1)} %copy.47) | data formatting | bytes 16777216 | tf_op jit(solution)/shard_map/reshape;reshape | solution.py:32
  424.1 12.0 %copy.48 = bf16[512,128,64]{1,2,0:T(8,128)(2,1)} copy(bf16[512,128,64]{1,0,2:T(8,128)(2,1)} %reshape_reshape.3) | data formatting | bytes 16777216 | tf_op jit(solution)/shard_map/reshape;reshape | solution.py:32
  436.1 4.1 gather_fusion
  440.3 0.0 copy-done
  440.3 0.0 copy-start.4
  440.3 1.5 convolution_bitcast_fusion.1
  441.8 0.0 copy-done.4
  441.8 0.0 copy-start.5
  441.8 2.0 fusion.10
  443.8 0.7 copy.74
  444.5 0.0 all-gather.3.cloned.1.call-update
  444.5 0.0 all-gather.5.cloned.1.call-start
  444.6 23.0 %all-gather.3.cloned.1.call-done = bf16[1024,512]{0,1:T(8,128)(2,1)} async-done(((bf16[1024,64]{0,1:T(8,128)(2,1)}), bf16[1024,512]{0,1:T(8,128)(2,1)}) %all-gather.3.cloned.1.call-update) | async-done | bytes 1048592 | tf_op jit(solution)/shard_map/all_gather | solution.py:39
  467.6 2.4 multiply_convert_fusion
  470.0 0.0 all-gather.5.cloned.1.call-update
  470.1 0.2 convert_reduce_fusion
  470.3 3.5 scatter_fusion
  473.8 0.7 copy.50
  474.5 15.4 %all-to-all-start.1 = ((s32[64,1,2]{2,1,0:T(1,128)}), s32[64,1,2]{2,1,0:T(1,128)S(1)}, u32[]{:S(2)}, u32[]{:S(2)}) async-start(s32[64,1,2]{2,1,0:T(1,128)} %copy.50), calls=%async_computation.1 | async-start | bytes 65536 | tf_op jit(solution)/shard_map/all_to_all | solution.py:75
  489.9 11.4 %all-gather.5.cloned.1.call-done = bf16[1024,512]{0,1:T(8,128)(2,1)} async-done(((bf16[1024,64]{0,1:T(8,128)(2,1)}), bf16[1024,512]{0,1:T(8,128)(2,1)}) %all-gather.5.cloned.1.call-update) | async-done | bytes 1048592 | tf_op jit(solution)/shard_map/all_gather | solution.py:50
  501.3 1.6 fusion.13
  502.9 0.7 gather_fusion.1
  503.7 2.0 convolution_bitcast_fusion
  505.7 2.5 broadcast_in_dim.10
  508.2 10.8 %scatter_fusion.1 = f32[64,2,128,64]{2,3,1,0:T(8,128)} fusion(f32[64,2,128,64]{2,3,1,0:T(8,128)} %broadcast_in_dim.10, s32[64]{0:T(128)S(1)} %fusion.31, f32[64,128,64]{1,2,0:T(8,128)} %convolution_bitcast_fusion), kind=kCustom, calls=%fused_computation.3 | custom fusion | bytes 6291968 | tf_op jit(solution)/shard_map/scatter | solution.py:66
  519.0 2.7 convert_element_type.49
  521.7 3.5 copy.53
  525.2 0.0 all-to-all-done.1
  525.2 15.7 %all-to-all-start.2 = ((bf16[64,2,128,64]{2,1,3,0:T(2,128)(2,1)}), bf16[64,2,128,64]{2,1,3,0:T(2,128)(2,1)}, u32[]{:S(2)}, u32[]{:S(2)}) async-start(bf16[64,2,128,64]{2,1,3,0:T(2,128)(2,1)} %copy.53), calls=%async_computation.2 | async-start | bytes 4194304 | tf_op jit(solution)/shard_map/all_to_all | solution.py:72
  540.9 0.0 all-reduce.2.cloned.1.call-start
  541.0 1.1 fusion.33
  542.1 0.0 all-reduce.2.cloned.1.call-update
  542.1 0.1 copy.51
  542.2 283.8 %all-reduce.2.cloned.1.call-done = f32[512,64]{0,1:T(8,128)} async-done(((f32[512,64]{0,1:T(8,128)}), f32[512,64]{0,1:T(8,128)}) %all-reduce.2.cloned.1.call-update) | async-done | bytes 131088 | tf_op jit(solution)/shard_map/psum | solution.py:55
  826.0 1.6 broadcast_multiply_fusion
  827.6 0.0 all-to-all-done.2
  827.6 3.8 abs_reduce_fusion
  831.4 0.1 copy.54
  831.5 4.5 fusion.7
  836.1 0.7 copy.73
  (16 shorter events, 0.1 us)
Async XLA Ops:
  7.2 433.1 %copy-start = (bf16[64,128,128]{2,1,0:T(8,128)(2,1)S(1)}, bf16[64,128,128]{2,1,0:T(8,128)(2,1)}, u32[]{:S(2)}) copy-start(bf16[64,128,128]{2,1,0:T(8,128)(2,1)} %param.9) | copy-start | bytes 6291460
  12.5 19.2 %copy-start.3 = (s32[64]{0:T(128)S(1)}, s32[64]{0:T(128)}, u32[]{:S(2)}) copy-start(s32[64]{0:T(128)} %param.12) | copy-start | bytes 772
  12.5 19.2 %copy-start.6 = (s32[64,1]{0,1:T(1,128)S(1)}, s32[64,1]{0,1:T(1,128)}, u32[]{:S(2)}) copy-start(s32[64,1]{0,1:T(1,128)} %param.11) | copy-start | bytes 772
  12.5 386.9 %all-to-all-start = ((bf16[64,1024,64]{1,2,0:T(8,128)(2,1)}), bf16[64,1024,64]{1,2,0:T(8,128)(2,1)}, u32[]{:S(2)}, u32[]{:S(2)}) async-start(bf16[64,1024,64]{1,2,0:T(8,128)(2,1)} %stack.2), calls=%async_computation | async-start | bytes 16777216 | tf_op jit(solution)/shard_map/all_to_all | solution.py:29
  31.7 435.9 %all-gather.3.cloned.1.call-start = ((), (), s32[]{:S(2)}) async-start(), calls=%async_computation.3 | async-start | bytes 1179648 | tf_op jit(solution)/shard_map/all_gather | solution.py:39
  440.3 1.5 copy-start.4
  441.8 25.8 %copy-start.5 = (s32[1024]{0:T(1024)S(1)}, s32[1024]{0:T(1024)}, u32[]{:S(2)}) copy-start(s32[1024]{0:T(1024)} %param.13) | copy-start | bytes 12292
  444.5 56.8 %all-gather.5.cloned.1.call-start = ((), (), s32[]{:S(2)}) async-start(), calls=%async_computation.5 | async-start | bytes 1179648 | tf_op jit(solution)/shard_map/all_gather | solution.py:50
  474.5 50.7 %all-to-all-start.1 = ((s32[64,1,2]{2,1,0:T(1,128)}), s32[64,1,2]{2,1,0:T(1,128)S(1)}, u32[]{:S(2)}, u32[]{:S(2)}) async-start(s32[64,1,2]{2,1,0:T(1,128)} %copy.50), calls=%async_computation.1 | async-start | bytes 65536 | tf_op jit(solution)/shard_map/all_to_all | solution.py:75
  525.1 15.8 %copy-start.1 = (bf16[1024,512]{0,1:T(8,128)(2,1)S(1)}, bf16[1024,512]{0,1:T(8,128)(2,1)}, u32[]{:S(2)}) copy-start(bf16[1024,512]{0,1:T(8,128)(2,1)} %all-gather.3.cloned.1.call-done) | copy-start | bytes 3145732
  525.1 15.8 %copy-start.2 = (bf16[1024,64]{0,1:T(8,128)(2,1)S(1)}, bf16[1024,64]{0,1:T(8,128)(2,1)}, u32[]{:S(2)}) copy-start(bf16[1024,64]{0,1:T(8,128)(2,1)} %get-tuple-element.3) | copy-start | bytes 393220
  525.2 302.4 %all-to-all-start.2 = ((bf16[64,2,128,64]{2,1,3,0:T(2,128)(2,1)}), bf16[64,2,128,64]{2,1,3,0:T(2,128)(2,1)}, u32[]{:S(2)}, u32[]{:S(2)}) async-start(bf16[64,2,128,64]{2,1,3,0:T(2,128)(2,1)} %copy.53), calls=%async_computation.2 | async-start | bytes 4194304 | tf_op jit(solution)/shard_map/all_to_all | solution.py:72
  540.9 285.1 %all-reduce.2.cloned.1.call-start = ((), (), s32[]{:S(2)}) async-start(), calls=%async_computation.4 | async-start | bytes 262144 | tf_op jit(solution)/shard_map/psum | solution.py:55
Sparse Core Ops, SparseCore 0:
  444.6 22.9 all-gather.2
  470.3 30.9 all-gather.4
  545.7 280.2 all-reduce.1
